TPU v7x, 256 devices: a whole 4x4x8 slice. The times are simulated.
256 devices in a mesh: seq: 32 (over y, z), wide: 8 (over x, core).
Axes of the slice: x: 4, y: 4, z: 8, core: 2. Of those that a mesh axis runs over, the one named last changes fastest.
Arguments:
- queries: bfloat16 [16384, 4096], P('seq', 'wide'), may hold values from -500 to 500
- keys: bfloat16 [16384, 4096], P('seq', 'wide'), may hold values from -500 to 500
- values: bfloat16 [16384, 4096], P('seq', 'wide'), may hold values from -6 to 6
- log_decay: float32 [16384, 32], P('seq', 'wide'), may hold values from -0.8 to 0, as said below
- ridge: float32 [4096], P('wide'), may hold values from 0.05 to 2
- out_weight: bfloat16 [4096, 4096], P('wide'), may hold values from -0.09375 to 0.09375
Outputs:
- mixed: bfloat16 [16384, 4096], P(('seq', 'wide'))
Inputs may be any that keep to these rules, and one draw needn't show every extreme that they name: `log_decay`: negative.
All inputs are finite; a program needn't handle non-finite values.
Results may differ from a plain program's by a relative error of at most 0.0065.
Values sent between devices are 32-bit elements; how exact they have to be, the bound alone decides.
A program may use at most 128 MiB of HBM per device.

v0:
```python
import jax
import jax.numpy as jnp
from jax import lax
from jax.sharding import PartitionSpec as P

HD = 128
SPAN = 128
ITERS = 8
highest = lax.Precision.HIGHEST


def unit_rows(matrix, head_count, head_size):
    entries = matrix.astype(jnp.float32).reshape(matrix.shape[0], head_count, head_size)
    return entries * lax.rsqrt(jnp.sum(entries * entries, axis=-1, keepdims=True) + 1e-06)


def span_read(query, key_rows, value_rows, cumulative, state_h, state_g, ridge_rows):
    length = query.shape[-2]
    places = jnp.arange(length)
    causal = places[:, None] >= places[None, :]
    spread = cumulative[..., :, None] - cumulative[..., None, :]
    weight = jnp.where(causal, jnp.exp(jnp.where(causal, spread, 0.0)), 0.0)
    opening = jnp.exp(cumulative)[..., None]
    solved = jnp.zeros_like(query)
    residual = query
    direction = query
    norm_now = jnp.sum(residual * residual, axis=-1, keepdims=True)
    for sweep in range(ITERS):
        operate_scores = (
            jnp.einsum("...td,...sd->...ts", direction, key_rows, precision=highest) * weight
        )
        operate_carried = jnp.einsum("...td,...ed->...te", direction, state_h, precision=highest)
        local_part = jnp.einsum("...ts,...sd->...td", operate_scores, key_rows, precision=highest)
        image = opening * operate_carried + local_part + ridge_rows * direction
        alpha = norm_now / jnp.sum(direction * image, axis=-1, keepdims=True)
        solved = solved + alpha * direction
        residual = residual - alpha * image
        norm_next = jnp.sum(residual * residual, axis=-1, keepdims=True)
        direction = residual + norm_next / norm_now * direction
        norm_now = norm_next
    scores = jnp.einsum("...td,...sd->...ts", solved, key_rows, precision=highest) * weight
    carried = jnp.einsum("...td,...ed->...te", solved, state_g, precision=highest)
    return opening * carried + jnp.einsum(
        "...ts,...se->...te", scores, value_rows, precision=highest
    )


def span_summary(key_rows, value_rows, cumulative):
    closing = cumulative[..., -1]
    fading = jnp.exp(closing[..., None] - cumulative)[..., None]
    gram = jnp.einsum("...sd,...se->...de", key_rows * fading, key_rows, precision=highest)
    memory = jnp.einsum("...se,...sd->...ed", value_rows * fading, key_rows, precision=highest)
    return (closing, gram, memory)


def combine_memories(earlier, later):
    factor = jnp.exp(later[2])[:, None, None]
    return (factor * earlier[0] + later[0], factor * earlier[1] + later[1], earlier[2] + later[2])


def body(queries, keys, values, log_decay, ridge, out_weight):
    rows_dev = queries.shape[0]
    head_count = log_decay.shape[1]
    head_size = HD
    block_list = rows_dev // SPAN

    def arrange(entries):
        return entries.reshape(block_list, SPAN, head_count, head_size).transpose(2, 0, 1, 3)

    query_rows = arrange(unit_rows(queries, head_count, head_size))
    key_rows = arrange(unit_rows(keys, head_count, head_size))
    value_rows = arrange(values.astype(jnp.float32).reshape(rows_dev, head_count, head_size))
    cumulative = jnp.cumsum(
        log_decay.reshape(block_list, SPAN, head_count).transpose(2, 0, 1), axis=-1
    )
    ridge_rows = ridge.reshape(head_count, 1, 1, head_size)
    closing, gram, memory = span_summary(key_rows, value_rows, cumulative)

    def running_summation(carry, items):
        return (combine_memories(carry, items), carry)

    blank_state = jnp.zeros((head_count, head_size, head_size), jnp.float32)
    blank_decay = jnp.zeros((head_count,), jnp.float32)
    shard_resident_carry, before = lax.scan(
        running_summation,
        (blank_state, blank_state, blank_decay),
        (gram.transpose(1, 0, 2, 3), memory.transpose(1, 0, 2, 3), closing.T),
    )
    device_h, device_g, device_decay = shard_resident_carry
    preceding_memory_h, incoming_gram_matrix, before_decay = before
    totals = lax.all_gather(device_decay[None], "seq", axis=0, tiled=True)
    position = lax.axis_index("seq")
    inclusive = jnp.cumsum(totals, axis=0)
    exclusive = inclusive - totals
    mine = lax.dynamic_index_in_dim(exclusive, position, 0, keepdims=False)
    preceding_rows = (jnp.arange(totals.shape[0]) < position)[:, None]
    lags = mine[None, :] - inclusive
    weights = jnp.where(preceding_rows, jnp.exp(jnp.where(preceding_rows, lags, 0.0)), 0.0)
    added_h = jnp.einsum(
        "jh,jhde->hde",
        weights,
        lax.all_gather(device_h[None], "seq", axis=0, tiled=True),
        precision=highest,
    )
    added_g = jnp.einsum(
        "jh,jhde->hde",
        weights,
        lax.all_gather(device_g[None], "seq", axis=0, tiled=True),
        precision=highest,
    )
    lifted = jnp.exp(before_decay)[..., None, None]
    start_h = (lifted * added_h[None] + preceding_memory_h).transpose(1, 0, 2, 3)
    start_g = (lifted * added_g[None] + incoming_gram_matrix).transpose(1, 0, 2, 3)
    reads = span_read(query_rows, key_rows, value_rows, cumulative, start_h, start_g, ridge_rows)
    reads = reads.transpose(1, 2, 0, 3).reshape(rows_dev, head_count, head_size)
    normed = reads * lax.rsqrt(jnp.mean(reads * reads, axis=-1, keepdims=True) + 1e-06)
    normed = normed.reshape(rows_dev, head_count * head_size).astype(jnp.bfloat16)
    mixed = lax.psum_scatter(
        jnp.dot(normed, out_weight, preferred_element_type=jnp.float32),
        "wide",
        scatter_dimension=0,
        tiled=True,
    )
    return mixed.astype(jnp.bfloat16)


def solution(mesh):
    placed = (
        P("seq", "wide"),
        P("seq", "wide"),
        P("seq", "wide"),
        P("seq", "wide"),
        P("wide"),
        P("wide", None),
    )
    return jax.shard_map(
        body, mesh=mesh, in_specs=placed, out_specs=P(("seq", "wide"), None), check_vma=False
    )
```

profile of v0, /device:TPU:1, one launch (start us, length us, event | category | flops | bytes accessed | tf_op | source)
XLA Modules:
  0.0 367.5 jit_solution(1191460066784433861)
XLA Ops:
  15.6 2.3 fusion.10
  17.9 3.2 convolution_bitcast_fusion.1
  23.5 8.0 %while.21 = (s32[]{:T(128)}, f32[4,128,128]{2,1,0:T(8,128)S(1)}, f32[4,128,128]{2,1,0:T(8,128)S(1)}, f32[4]{0:T(128)S(1)}, f32[4,4,128,128]{3,2,1,0:T(8,128)}, /...) while((s32[]{:T(128)}, f32[4,128,128]{2,1,0:T(8,128)S(1)}, ...), condition=%wide.region_5.6_spmd.clone, body=%wide.region_4.5_spmd.clone.sunk | while | flops 524299 | bytes 2622221 | solution.py:84
  34.4 65.5 %all-reduce = f32[128]{0:T(128)S(1)} all-reduce(f32[128]{0:T(128)S(1)} %dynamic-update-slice), channel_id=2, replica_groups=mesh['seq'=32,'wide'=8] {'seq'}, use_global_device_ids=true, to_apply=%add | all-reduce | flops 128 | bytes 1024
  100.2 2.4 reshape.176
  102.6 2.2 convert_multiply_fusion.1
  108.8 3.0 convolution_multiply_fusion.15
  111.8 21.4 %all-gather.6.cloned.1.call-done = f32[128,128,128]{2,1,0:T(8,128)} async-done(((f32[4,128,128]{2,1,0:T(8,128)}), f32[128,128,128]{2,1,0:T(8,128)}) %all-gather.6.cloned.1.call-update) | async-done | bytes 8388624 | tf_op jit(solution)/shard_map/all_gather | solution.py:102
  133.3 12.0 %fusion.6 = f32[4,1,128,128]{3,1,2,0:T(1,128)S(1)} fusion(f32[32,4,1,1]{0,2,3,1:T(1,128)S(1)} %copy.109, f32[32,4,128,128]{3,2,1,0:T(8,128)} %bitcast.204), kind=kOutput, calls=%fused_computation.12 | convolution fusion | flops 25165824 | bytes 8651264 | tf_op jit(solution)/shard_map/jh,jhde->hde/dot_general | solution.py:99
  145.3 85.5 %all-gather.8.cloned.1.call-done = f32[128,128,128]{2,1,0:T(8,128)} async-done(((f32[4,128,128]{2,1,0:T(8,128)}), f32[128,128,128]{2,1,0:T(8,128)}) %all-gather.8.cloned.1.call-update) | async-done | bytes 8388624 | tf_op jit(solution)/shard_map/all_gather | solution.py:108
  230.8 12.3 %fusion.4 = f32[4,1,128,128]{3,1,2,0:T(1,128)S(1)} fusion(f32[32,4,1,1]{0,2,3,1:T(1,128)S(1)} %copy.109, f32[32,4,128,128]{3,2,1,0:T(8,128)} %bitcast.205), kind=kOutput, calls=%fused_computation.10 | convolution fusion | flops 25165824 | bytes 8651264 | tf_op jit(solution)/shard_map/jh,jhde->hde/dot_general | solution.py:105
  244.7 2.5 fusion.48
  247.7 2.1 convolution_multiply_fusion.13
  251.0 2.4 multiply_reduce_fusion.12
  257.8 2.4 multiply_reduce_fusion.10
  263.9 2.4 multiply_reduce_fusion.8
  270.0 2.6 multiply_reduce_fusion.6
  276.3 2.4 multiply_reduce_fusion.4
  279.1 2.1 convolution_multiply_fusion.3
  282.4 2.4 multiply_reduce_fusion.2
  285.5 2.3 convolution_multiply_fusion.1
  289.0 2.4 fusion.24
  298.5 7.8 %fusion.70 = f32[512,4096]{1,0:T(8,128)} fusion(bf16[512,4096]{1,0:T(8,128)(2,1)} %param.13, f32[64,8,4,128]{3,2,1,0:T(4,128)S(1)} %bitcast.206, f32[64,8,4,128]{3,2,1,0:T(4,128)S(1)} %bitcast.207), kind=kOutput, calls=%fused_computation.138 | convolution fusion | flops 2148007936 | bytes 14680064 | tf_op jit(solution)/shard_map/dot_general | solution.py:119
  306.3 52.4 %reduce-scatter.2.cloned.1.call-done = f32[64,4096]{1,0:T(8,128)} async-done(((f32[512,4096]{1,0:T(8,128)}), f32[64,4096]{1,0:T(8,128)}) %reduce-scatter.2.cloned.1.call-update) | async-done | bytes 1048592 | tf_op jit(solution)/shard_map/reduce_scatter | solution.py:118
  (125 shorter events, 56.9 us)
Async XLA Ops:
  6.5 8.6 %copy-start.5 = (bf16[512,512]{1,0:T(8,128)(2,1)S(1)}, bf16[512,512]{1,0:T(8,128)(2,1)}, u32[]{:S(2)}) copy-start(bf16[512,512]{1,0:T(8,128)(2,1)} %param.10) | copy-start | bytes 1572868
  6.5 126.7 %all-gather.6.cloned.1.call-start = ((), (), s32[]{:S(2)}) async-start(), calls=%async_computation.2 | async-start | bytes 8650752 | tf_op jit(solution)/shard_map/all_gather | solution.py:102
  21.1 11.8 %copy-start.7 = (u32[256]{0:T(256)S(1)}, u32[256]{0:T(256)}, u32[]{:S(2)}) copy-start(u32[256]{0:T(256)} %constant.48) | copy-start | bytes 3076
  31.4 0.7 copy-start
  31.4 0.8 copy-start.1
  32.1 198.7 %all-gather.8.cloned.1.call-start = ((), (), s32[]{:S(2)}) async-start(), calls=%async_computation.3 | async-start | bytes 8650752 | tf_op jit(solution)/shard_map/all_gather | solution.py:108
  32.9 325.8 %reduce-scatter.2.cloned.1.call-start = ((), (), s32[]{:S(2)}) async-start(), calls=%async_computation.1 | async-start | bytes 9437184 | tf_op jit(solution)/shard_map/reduce_scatter | solution.py:118
  145.3 99.4 %copy-start.6 = (f32[512]{0:T(512)S(1)}, f32[512]{0:T(512)}, u32[]{:S(2)}) copy-start(f32[512]{0:T(512)} %param.12) | copy-start | bytes 6148
  230.8 12.3 %copy-start.3 = (f32[4,4,128,128]{3,2,1,0:T(8,128)S(1)}, f32[4,4,128,128]{3,2,1,0:T(8,128)}, u32[]{:S(2)}) copy-start(f32[4,4,128,128]{3,2,1,0:T(8,128)} %get-tuple-element.65) | copy-start | bytes 3145732
  230.8 12.4 %copy-start.4 = (f32[4,4,128,128]{3,2,1,0:T(8,128)S(1)}, f32[4,4,128,128]{3,2,1,0:T(8,128)}, u32[]{:S(2)}) copy-start(f32[4,4,128,128]{3,2,1,0:T(8,128)} %get-tuple-element.67) | copy-start | bytes 3145732
  230.8 13.9 %copy-start.2 = (f32[4,4,128,128]{3,2,1,0:T(8,128)S(1)}, f32[4,4,128,128]{3,2,1,0:T(8,128)}, u32[]{:S(2)}) copy-start(f32[4,4,128,128]{3,2,1,0:T(8,128)} %convolution_multiply_fusion.15) | copy-start | bytes 3145732
Sparse Core Ops, SparseCore 0:
  32.3 100.9 all-gather.5
  135.9 94.9 all-gather.7
  306.4 52.2 reduce-scatter.1
where the time goes:
time: 373 us; the launch traced here: 368 us
  waiting for transfers between devices  160 us (43%)
  matrix products  89.4 us (24%)
  blocking collectives  65.5 us (18%)
  other arithmetic  22.3 us (6%)
  local copies, waits for them, and re-layouts  15.6 us (4%)
  between operations  14.5 us (4%)
    all_gather x1, waiting for transfers between devices, body(): lax.all_gather(device_g[None], 'seq', axis=0, tiled=True)  85.5 us
    unnamed x1, blocking collectives  65.5 us
    reduce_scatter x1, waiting for transfers between devices, body(): lax.psum_scatter(jnp.dot(normed, out_weight, preferred_element_type=jnp.f...  52.4 us
    all_gather x1, waiting for transfers between devices, body(): lax.all_gather(device_h[None], 'seq', axis=0, tiled=True)  21.4 us
    dot_general x8, matrix products, span_read(): jnp.einsum('...ts,...sd->...td', operate_scores, key_rows, precision=high...  19.5 us
    dot_general x8, matrix products, span_read(): jnp.einsum('...td,...sd->...ts', direction, key_rows, precision=highest)  18.1 us
    dot_general x1, matrix products, body(): jnp.einsum('jh,jhde->hde', weights, lax.all_gather(device_g[None], 'seq',...  12.3 us
    dot_general x1, matrix products, body(): jnp.einsum('jh,jhde->hde', weights, lax.all_gather(device_h[None], 'seq',...  12 us
  transfers between devices with their start and end apart: 3, of which 3 were waited for; matrix products, arithmetic and copies ran while one was open for 7% of the time, Pallas kernels for 0%

commit v1 on v0

--- a/solution.py
+++ b/solution.py
@@ -105,7 +105,9 @@
     added_g = jnp.einsum(
         "jh,jhde->hde",
         weights,
-        lax.all_gather(device_g[None], "seq", axis=0, tiled=True),
+        jnp.concatenate(
+            lax.all_to_all(jnp.stack([device_g[None]] * lax.axis_size("seq")), "seq", 0, 0), axis=0
+        ),
         precision=highest,
     )
     lifted = jnp.exp(before_decay)[..., None, None]

time: 373 us -> 509 us (1.36)
  blocking collectives: 65.5 us -> 285 us
  waiting for transfers between devices: 160 us -> 61.6 us
  starting transfers between devices: 0.08 us -> 12.3 us
    unnamed x1, blocking collectives: 65.5 us -> 285 us
    all_gather x1 -> x0, waiting for transfers between devices: 85.5 us -> none  [body(): lax.all_gather(device_g[None], 'seq', axis=0, tiled=True)]
    all_gather x1, waiting for transfers between devices: 21.4 us -> 0.01 us  [body(): lax.all_gather(device_h[None], 'seq', axis=0, tiled=True)]
    all_to_all x0 -> x1, starting transfers between devices: none -> 12.3 us  [body(): lax.all_to_all(jnp.stack([device_g[None]] * lax.axis_size('seq')), 'seq',...]
    reduce_scatter x1, waiting for transfers between devices: 52.4 us -> 61.6 us  [body(): lax.psum_scatter(jnp.dot(normed, out_weight, preferred_element_type=jnp.f...]
  transfers between devices with their start and end apart: 3 -> 3, of which waited for: 3 -> 1; matrix products, arithmetic and copies ran while one was open for 7% -> 5% of each run, Pallas kernels for 0% -> 0%
where the time goes in v1:
time: 509 us; the launch traced here: 503 us
  blocking collectives  285 us (56%)
  matrix products  89.6 us (18%)
  waiting for transfers between devices  61.6 us (12%)
  other arithmetic  21.2 us (4%)
  local copies, waits for them, and re-layouts  18.8 us (4%)
  between operations  14.8 us (3%)
  starting transfers between devices  12.3 us (2%)
    unnamed x1, blocking collectives  285 us
    reduce_scatter x1, waiting for transfers between devices, body(): lax.psum_scatter(jnp.dot(normed, out_weight, preferred_element_type=jnp.f...  61.6 us
    dot_general x8, matrix products, span_read(): jnp.einsum('...ts,...sd->...td', operate_scores, key_rows, precision=high...  19.8 us
    dot_general x8, matrix products, span_read(): jnp.einsum('...td,...sd->...ts', direction, key_rows, precision=highest)  18.1 us
    dot_general x1, matrix products, body(): jnp.einsum('jh,jhde->hde', weights, jnp.concatenate(lax.all_to_all(jnp.st...  12.4 us
    all_to_all x1, starting transfers between devices, body(): lax.all_to_all(jnp.stack([device_g[None]] * lax.axis_size('seq')), 'seq',...  12.3 us
    dot_general x1, matrix products, body(): jnp.einsum('jh,jhde->hde', weights, lax.all_gather(device_h[None], 'seq',...  12 us
  transfers between devices with their start and end apart: 3, of which 1 were waited for; matrix products, arithmetic and copies ran while one was open for 5% of the time, Pallas kernels for 0%

profile of v1, /device:TPU:1, one launch (start us, length us, event | category | flops | bytes accessed | tf_op | source)
XLA Modules:
  0.0 503.1 jit_solution(8088460955005720548)
XLA Ops:
  15.6 2.3 fusion.10
  17.9 3.2 convolution_bitcast_fusion.1
  23.4 7.9 %while.21 = (s32[]{:T(128)}, f32[4,128,128]{2,1,0:T(8,128)S(1)}, f32[4,128,128]{2,1,0:T(8,128)S(1)}, f32[4]{0:T(128)S(1)}, f32[4,4,128,128]{3,2,1,0:T(8,128)}, /...) while((s32[]{:T(128)}, f32[4,128,128]{2,1,0:T(8,128)S(1)}, ...), condition=%wide.region_5.6_spmd.clone, body=%wide.region_4.5_spmd.clone.sunk | while | flops 524299 | bytes 2622221 | solution.py:84
  32.1 4.3 stack.3
  36.3 12.3 %all-to-all-start = ((f32[32,1,4,128,128]{4,3,2,1,0:T(8,128)}), f32[32,1,4,128,128]{4,3,2,1,0:T(8,128)}, u32[]{:S(2)}, u32[]{:S(2)}) async-start(f32[32,1,4,128,128]{4,3,2,1,0:T(8,128)} %stack.3), calls=%async_computation | async-start | bytes 16777216 | tf_op jit(solution)/shard_map/all_to_all | solution.py:109
  50.2 284.7 %all-reduce = f32[128]{0:T(128)S(1)} all-reduce(f32[128]{0:T(128)S(1)} %dynamic-update-slice), channel_id=2, replica_groups=mesh['seq'=32,'wide'=8] {'seq'}, use_global_device_ids=true, to_apply=%add | all-reduce | flops 128 | bytes 1024
  341.7 3.1 convolution_multiply_fusion.15
  344.8 12.0 %fusion.6 = f32[4,1,128,128]{3,1,2,0:T(1,128)S(1)} fusion(f32[32,4,1,1]{0,2,3,1:T(1,128)S(1)} %copy.109, f32[32,4,128,128]{3,2,1,0:T(8,128)} %bitcast.204), kind=kOutput, calls=%fused_computation.12 | convolution fusion | flops 25165824 | bytes 8651264 | tf_op jit(solution)/shard_map/jh,jhde->hde/dot_general | solution.py:99
  356.9 12.4 %fusion.4 = f32[4,1,128,128]{3,1,2,0:T(1,128)S(1)} fusion(f32[32,4,1,1]{0,2,3,1:T(1,128)S(1)} %copy.109, f32[32,4,128,128]{3,2,1,0:T(8,128)} %bitcast.18), kind=kOutput, calls=%fused_computation.10 | convolution fusion | flops 25165824 | bytes 8651264 | tf_op jit(solution)/shard_map/jh,jhde->hde/dot_general | solution.py:105
  370.7 2.5 fusion.48
  373.8 2.1 convolution_multiply_fusion.13
  377.1 2.4 multiply_reduce_fusion.12
  383.7 2.4 multiply_reduce_fusion.10
  386.5 2.1 convolution_multiply_fusion.9
  389.8 2.4 multiply_reduce_fusion.8
  392.6 2.1 convolution_multiply_fusion.7
  395.9 2.9 multiply_reduce_fusion.6
  402.5 2.4 multiply_reduce_fusion.4
  405.3 2.1 convolution_multiply_fusion.3
  408.6 2.4 multiply_reduce_fusion.2
  411.6 2.3 convolution_multiply_fusion.1
  415.1 2.4 fusion.24
  424.6 7.8 %fusion.70 = f32[512,4096]{1,0:T(8,128)} fusion(bf16[512,4096]{1,0:T(8,128)(2,1)} %param.13, f32[64,8,4,128]{3,2,1,0:T(4,128)S(1)} %bitcast.205, f32[64,8,4,128]{3,2,1,0:T(4,128)S(1)} %bitcast.206), kind=kOutput, calls=%fused_computation.138 | convolution fusion | flops 2148007936 | bytes 14680064 | tf_op jit(solution)/shard_map/dot_general | solution.py:121
  432.4 61.6 %reduce-scatter.2.cloned.1.call-done = f32[64,4096]{1,0:T(8,128)} async-done(((f32[512,4096]{1,0:T(8,128)}), f32[64,4096]{1,0:T(8,128)}) %reduce-scatter.2.cloned.1.call-update) | async-done | bytes 1048592 | tf_op jit(solution)/shard_map/reduce_scatter | solution.py:120
  (125 shorter events, 54.1 us)
Async XLA Ops:
  6.5 8.6 %copy-start.5 = (bf16[512,512]{1,0:T(8,128)(2,1)S(1)}, bf16[512,512]{1,0:T(8,128)(2,1)}, u32[]{:S(2)}) copy-start(bf16[512,512]{1,0:T(8,128)(2,1)} %param.10) | copy-start | bytes 1572868
  6.5 338.3 %all-gather.4.cloned.1.call-start = ((), (), s32[]{:S(2)}) async-start(), calls=%async_computation.3 | async-start | bytes 8650752 | tf_op jit(solution)/shard_map/all_gather | solution.py:102
  31.3 0.7 copy-start
  36.3 12.4 %copy-start.7 = (u32[256]{0:T(256)S(1)}, u32[256]{0:T(256)}, u32[]{:S(2)}) copy-start(u32[256]{0:T(256)} %constant.48) | copy-start | bytes 3076
  36.3 298.9 %copy-start.4 = (bf16[512,512]{1,0:T(8,128)(2,1)S(1)}, bf16[512,512]{1,0:T(8,128)(2,1)}, u32[]{:S(2)}) copy-start(bf16[512,512]{1,0:T(8,128)(2,1)} %param.8) | copy-start | bytes 1572868
  36.3 320.5 %all-to-all-start = ((f32[32,1,4,128,128]{4,3,2,1,0:T(8,128)}), f32[32,1,4,128,128]{4,3,2,1,0:T(8,128)}, u32[]{:S(2)}, u32[]{:S(2)}) async-start(f32[32,1,4,128,128]{4,3,2,1,0:T(8,128)} %stack.3), calls=%async_computation | async-start | bytes 16777216 | tf_op jit(solution)/shard_map/all_to_all | solution.py:109
  48.6 445.3 %reduce-scatter.2.cloned.1.call-start = ((), (), s32[]{:S(2)}) async-start(), calls=%async_computation.2 | async-start | bytes 9437184 | tf_op jit(solution)/shard_map/reduce_scatter | solution.py:120
  356.8 13.9 %copy-start.6 = (f32[512]{0:T(512)S(1)}, f32[512]{0:T(512)}, u32[]{:S(2)}) copy-start(f32[512]{0:T(512)} %param.12) | copy-start | bytes 6148
  356.8 12.4 %copy-start.2 = (f32[4,4,128,128]{3,2,1,0:T(8,128)S(1)}, f32[4,4,128,128]{3,2,1,0:T(8,128)}, u32[]{:S(2)}) copy-start(f32[4,4,128,128]{3,2,1,0:T(8,128)} %get-tuple-element.65) | copy-start | bytes 3145732
  356.8 12.4 %copy-start.3 = (f32[4,4,128,128]{3,2,1,0:T(8,128)S(1)}, f32[4,4,128,128]{3,2,1,0:T(8,128)}, u32[]{:S(2)}) copy-start(f32[4,4,128,128]{3,2,1,0:T(8,128)} %get-tuple-element.67) | copy-start | bytes 3145732
  356.9 13.9 %copy-start.1 = (f32[4,4,128,128]{3,2,1,0:T(8,128)S(1)}, f32[4,4,128,128]{3,2,1,0:T(8,128)}, u32[]{:S(2)}) copy-start(f32[4,4,128,128]{3,2,1,0:T(8,128)} %convolution_multiply_fusion.15) | copy-start | bytes 3145732
Sparse Core Ops, SparseCore 0:
  32.2 213.3 all-gather.3
  432.5 61.4 reduce-scatter.1
